TPU v7x, 256 devices: a whole 4x4x8 slice. The times are simulated.
256 devices in a mesh: pix: 64 (over x, z, core), band: 4 (over y).
Axes of the slice: x: 4, y: 4, z: 8, core: 2. Of those that a mesh axis runs over, the one named last changes fastest.
Arguments:
- spectra: bfloat16 [224, 262144], P('band', 'pix'), may hold values from -0.1 to 4
- endmembers: bfloat16 [224, 512], P('band'), may hold values from 0.05 to 1
- gram_inverse: float32 [512, 512], replicated, may hold values from -1 to 1, as said below
- abundances: float32 [512, 262144], P(None, ('pix', 'band')), may hold values from 0 to 512, as said below
- duals: float32 [512, 262144], P(None, ('pix', 'band')), may hold values from -4 to 4
Outputs:
- abundances_out: float32 [512, 262144], P(None, ('pix', 'band'))
- duals_out: float32 [512, 262144], P(None, ('pix', 'band'))
- residual_rms: float32 [2, 2], replicated
Inputs may be any that keep to these rules, and one draw needn't show every extreme that they name: `abundances`: each column is nonnegative and sums to 512. `gram_inverse`: penalty times the float32 inverse of endmembers^T endmembers / 512^2 + penalty I, with penalty = 224 / (2 * 512^2) and the endmembers as stored.
All inputs are finite; a program needn't handle non-finite values.
Results may differ from a plain program's by a relative error of at most 0.0004.
Values may be sent and summed in bfloat16 or wider, within the bound.
A program may use at most 64 MiB of HBM per device.

v0:
```python
import jax
import jax.numpy as jnp
from jax import lax
from jax.sharding import Mesh
from jax.sharding import PartitionSpec as P

B = 224
K = 512
ITERS = 2
BISECT = 6
PIX = ("pix_0", "pix_1", "pix_2")
PIX_BAND = ("pix_0", "pix_1", "pix_2", "band")


def one_axis_at_a_time(shard, axes):
    for axis in axes:
        shard = lax.psum(shard, axis)
    return shard


def project(shifted):
    simplex_sum = float(K)
    high_end = jnp.max(shifted, axis=0)
    low_end = (jnp.sum(shifted, axis=0) - simplex_sum) / simplex_sum

    def mass_at(level):
        return jnp.sum(jnp.maximum(shifted - level[None, :], 0.0), axis=0)

    mass_low = mass_at(low_end)
    mass_high = jnp.zeros_like(high_end)

    def bisect_once(unused, state):
        low_now, high_now, low_mass, high_mass = state
        middle = 0.5 * (low_now + high_now)
        total_mass = mass_at(middle)
        too_high = total_mass > simplex_sum
        return (
            jnp.where(too_high, middle, low_now),
            jnp.where(too_high, high_now, middle),
            jnp.where(too_high, total_mass, low_mass),
            jnp.where(too_high, high_mass, total_mass),
        )

    low_end, high_end, mass_low, mass_high = lax.fori_loop(
        0, BISECT, bisect_once, (low_end, high_end, mass_low, mass_high)
    )
    level = low_end + (mass_low - simplex_sum) * (high_end - low_end) / (mass_low - mass_high)
    return jnp.maximum(shifted - level[None, :], 0.0)


def contract_bands(signatures, columns):
    return lax.dot_general(
        signatures, columns, (((0,), (0,)), ((), ())), preferred_element_type=jnp.float32
    )


def body(spectra, endmembers, gram_inverse, abundances, duals):
    penalty = B / (2.0 * K * K)
    exchanged = lax.all_to_all(spectra, "band", split_axis=1, concat_axis=0, tiled=True)
    all_rows = lax.all_gather(endmembers, "band", axis=0, tiled=True)
    fit_term = contract_bands(all_rows, exchanged)
    fit_term = fit_term / K
    pixel_count = abundances.shape[1] * lax.axis_size(PIX) * lax.axis_size("band")
    current = abundances
    scaled_dual = duals
    primal_list = []
    change_list = []
    for sweep in range(ITERS):
        primal = jnp.dot(
            gram_inverse,
            fit_term / penalty + current - scaled_dual,
            precision=lax.Precision.HIGHEST,
        )
        updated = project(primal + scaled_dual)
        scaled_dual = scaled_dual + primal - updated
        primal_sum = jnp.sum((primal - updated) ** 2)
        change_sum = jnp.sum((updated - current) ** 2)
        primal_list.append(primal_sum)
        change_list.append(change_sum)
        current = updated
    totals = jnp.stack([jnp.stack(primal_list), jnp.stack(change_list)])
    totals = one_axis_at_a_time(totals, PIX_BAND)
    residual_rms = jnp.sqrt(totals / pixel_count)
    return (current, scaled_dual, residual_rms)


def solution(mesh):
    finer = Mesh(
        mesh.devices.reshape(4, 8, 2, mesh.shape["band"]), ("pix_0", "pix_1", "pix_2", "band")
    )
    return jax.shard_map(
        body,
        mesh=finer,
        in_specs=(P("band", PIX), P("band", None), P(), P(None, PIX_BAND), P(None, PIX_BAND)),
        out_specs=(P(None, PIX_BAND), P(None, PIX_BAND), P()),
        check_vma=False,
    )
```

profile of v0, /device:TPU:1, one launch (start us, length us, event | category | flops | bytes accessed | tf_op | source)
XLA Modules:
  0.0 109.2 jit_solution(441457199507730125)
XLA Ops:
  0.6 1.9 %copy.12 = bf16[7,4,8,1024]{3,2,0,1:T(8,128)(2,1)} copy(bf16[7,4,8,1024]{3,2,1,0:T(8,128)(2,1)} %bitcast.36) | data formatting | bytes 917504 | tf_op jit(solution)/shard_map/all_to_all | solution.py:59
  2.5 5.0 %all-to-all-start = ((bf16[56,4,1024]{2,0,1:T(8,128)(2,1)}), bf16[56,4,1024]{2,0,1:T(8,128)(2,1)S(1)}, u32[]{:S(2)}, u32[]{:S(2)}) async-start(bf16[56,4,1024]{2,0,1:T(8,128)(2,1)} %bitcast.34), calls=%async_computation | async-start | bytes 917504 | tf_op jit(solution)/shard_map/all_to_all | solution.py:59
  7.6 12.5 %all_gather.3 = bf16[224,512]{1,0:T(8,128)(2,1)S(1)} all-gather(bf16[56,512]{1,0:T(8,128)(2,1)} %param.10), channel_id=1, replica_groups=mesh['pix_0'=4,'pix_1'=8,'pix_2'=2,'band'=4] {'band'}, dimensions={0}, use_global_device_ids=true | all-gather | bytes 286720 | tf_op jit(solution)/shard_map/all_gather | solution.py:60
  20.0 0.5 fusion.29
  20.5 8.7 %fusion.28 = (f32[1024]{0:T(1024)S(1)}, f32[512,1024]{1,0:T(8,128)S(1)}, f32[1024,512]{0,1:T(8,128)}) fusion(f32[512,1024]{1,0:T(8,128)} %param.13, f32[512,512]{1,0:T(8,128)S(1)} %copy-done, f32[512,1024]{1,0:T(8,128)} %param.12, f32[512,1024]{1,0:T(8,128)S(1)} %fusion.29), kind=kOutput, calls=%fused_computation.54 | convolution fusion | flops 3223845888 | bytes 11538432 | tf_op jit(solution)/shard_map/dot_general | solution.py:69
  29.5 1.9 %while.34 = (s32[]{:T(128)}, f32[1024]{0:T(1024)S(1)}, f32[1024]{0:T(1024)S(1)}, f32[1024]{0:T(1024)S(1)}, f32[1024]{0:T(1024)S(1)}, /*index=5*/f32[512,1024]{1,0:T(8,128)S(1)}, s32[]{:T(128)}, s32[]{:T(128)}) while((s32[]{:T(128)}, f32[1024]{0:T(1024)S(1)}, f32[1024]{0:T(1024)S(1)}, f32[1024]{0:T(1024)S(1)}, f32[1024]{0:T(1024)S(1)}, ...), condition=%wide.region_5.6_spmd.clone, body=%wide.region_3.5_spmd.clone.sunk | while | flops 1582083 | bytes 2154591 | solution.py:44
  31.5 7.0 %fusion.27 = (f32[1024]{0:T(1024)S(1)}, f32[512,1024]{1,0:T(8,128)S(1)}, f32[1024,512]{0,1:T(8,128)}) fusion(f32[512,1024]{1,0:T(8,128)S(1)} %get-tuple-element.310, f32[1024]{0:T(1024)S(1)} %divide_add_fusion.1, f32[512,512]{1,0:T(8,128)S(1)} %copy-done, f32[512,1024]{1,0:T(8,128)} %copy-done.2), kind=kOutput, calls=%fused_computation.53 | convolution fusion | flops 3226991616 | bytes 9445376 | tf_op jit(solution)/shard_map/dot_general | solution.py:69
  38.5 0.3 maximum_reduce_fusion.2
  38.8 1.0 copy-done.1
  39.8 11.3 %while.35 = (s32[]{:T(128)}, f32[1024]{0:T(1024)S(1)}, f32[1024]{0:T(1024)S(1)}, f32[1024]{0:T(1024)S(1)}, f32[1024]{0:T(1024)S(1)}, /*index=5*/f32[512,1024]{1,0:T(8,128)}, s32[]{:T(128)}, s32[]{:T(128)}) while((s32[]{:T(128)}, f32[1024]{0:T(1024)S(1)}, f32[1024]{0:T(1024)S(1)}, f32[1024]{0:T(1024)S(1)}, f32[1024]{0:T(1024)S(1)}, ...), condition=%wide.region_11.12_spmd.clone, body=%wide.region_9.0_spmd.clone.sunk | while | flops 1582083 | bytes 2154591 | solution.py:44
  39.8 1.8 %maximum_reduce_fusion.7 = f32[1024]{0:T(1024)S(1)} fusion(f32[512,1024]{1,0:T(8,128)} %get-tuple-element.307, f32[1024]{0:T(1024)S(1)} %add_multiply_fusion.7), kind=kLoop, calls=%fused_computation.7.clone.1 | loop fusion | flops 1571840 | bytes 2105344 | tf_op jit(solution)/shard_map/while/body/eval_jaxpr/reduce_sum | solution.py:27
  41.7 1.8 %maximum_reduce_fusion.7 = f32[1024]{0:T(1024)S(1)} fusion(f32[512,1024]{1,0:T(8,128)} %get-tuple-element.307, f32[1024]{0:T(1024)S(1)} %add_multiply_fusion.7), kind=kLoop, calls=%fused_computation.7.clone.1 | loop fusion | flops 1571840 | bytes 2105344 | tf_op jit(solution)/shard_map/while/body/eval_jaxpr/reduce_sum | solution.py:27
  43.6 1.8 %maximum_reduce_fusion.7 = f32[1024]{0:T(1024)S(1)} fusion(f32[512,1024]{1,0:T(8,128)} %get-tuple-element.307, f32[1024]{0:T(1024)S(1)} %add_multiply_fusion.7), kind=kLoop, calls=%fused_computation.7.clone.1 | loop fusion | flops 1571840 | bytes 2105344 | tf_op jit(solution)/shard_map/while/body/eval_jaxpr/reduce_sum | solution.py:27
  45.5 1.8 %maximum_reduce_fusion.7 = f32[1024]{0:T(1024)S(1)} fusion(f32[512,1024]{1,0:T(8,128)} %get-tuple-element.307, f32[1024]{0:T(1024)S(1)} %add_multiply_fusion.7), kind=kLoop, calls=%fused_computation.7.clone.1 | loop fusion | flops 1571840 | bytes 2105344 | tf_op jit(solution)/shard_map/while/body/eval_jaxpr/reduce_sum | solution.py:27
  47.3 1.8 %maximum_reduce_fusion.7 = f32[1024]{0:T(1024)S(1)} fusion(f32[512,1024]{1,0:T(8,128)} %get-tuple-element.307, f32[1024]{0:T(1024)S(1)} %add_multiply_fusion.7), kind=kLoop, calls=%fused_computation.7.clone.1 | loop fusion | flops 1571840 | bytes 2105344 | tf_op jit(solution)/shard_map/while/body/eval_jaxpr/reduce_sum | solution.py:27
  49.2 1.8 %maximum_reduce_fusion.7 = f32[1024]{0:T(1024)S(1)} fusion(f32[512,1024]{1,0:T(8,128)} %get-tuple-element.307, f32[1024]{0:T(1024)S(1)} %add_multiply_fusion.7), kind=kLoop, calls=%fused_computation.7.clone.1 | loop fusion | flops 1571840 | bytes 2105344 | tf_op jit(solution)/shard_map/while/body/eval_jaxpr/reduce_sum | solution.py:27
  51.1 7.0 %fusion.9 = (f32[]{:T(128)}, f32[]{:T(128)}, f32[]{:T(128)}, f32[]{:T(128)}, f32[512,1024]{1,0:T(8,128)}) fusion(f32[1024,512]{0,1:T(8,128)} %get-tuple-element.168, f32[512,1024]{1,0:T(8,128)S(1)} %get-tuple-element.310, f32[1024]{0:T(1024)S(1)} %divide_add_fusion.1, f32[512,1024]{1,0:T(8,128)} %param.12, f32[1024,512]{0,1:T(8,128)} %get-tuple-element.169, ...), kind=kLoop, calls=%fused_computation.21 | loop fusion | flops 8388604 | bytes 12591120 | tf_op jit(solution)/shard_map/reduce_sum | solution.py:76
  58.1 2.6 %maximum_bitcast_fusion = (f32[1,2]{1,0:T(1,128)S(1)}, f32[1,2]{1,0:T(1,128)S(1)}) fusion(f32[1]{0:T(128)} %bitcast.5, f32[1]{0:T(128)} %bitcast.4, f32[1]{0:T(128)} %bitcast.8, f32[1]{0:T(128)} %bitcast.7), kind=kLoop, calls=%fused_computation.48 | loop fusion | flops 4 | bytes 32 | tf_op jit(solution)/shard_map/stack | solution.py:81
  60.7 8.0 %psum.28 = f32[2,2]{1,0:T(2,128)S(1)} all-reduce(f32[2,2]{1,0:T(2,128)S(1)} %pad_maximum_fusion), channel_id=1, replica_groups=mesh['pix_0'=4,'pix_1'=8,'pix_2'=2,'band'=4] {'pix_0'}, use_global_device_ids=true, to_apply=%region_16.17 | all-reduce | flops 4 | bytes 32 | tf_op jit(solution)/shard_map/psum | solution.py:17
  68.8 16.2 %psum.29 = f32[2,2]{1,0:T(2,128)S(1)} all-reduce(f32[2,2]{1,0:T(2,128)S(1)} %psum.28), channel_id=1, replica_groups=mesh['pix_0'=4,'pix_1'=8,'pix_2'=2,'band'=4] {'pix_1'}, use_global_device_ids=true, to_apply=%region_17.18 | all-reduce | flops 4 | bytes 32 | tf_op jit(solution)/shard_map/psum | solution.py:17
  85.0 12.4 %psum.30 = f32[2,2]{1,0:T(2,128)S(1)} all-reduce(f32[2,2]{1,0:T(2,128)S(1)} %psum.29), channel_id=1, replica_groups=mesh['pix_0'=4,'pix_1'=8,'pix_2'=2,'band'=4] {'pix_2'}, use_global_device_ids=true, to_apply=%region_18.19 | all-reduce | flops 4 | bytes 32 | tf_op jit(solution)/shard_map/psum | solution.py:17
  97.4 7.1 %psum.31 = f32[2,2]{1,0:T(2,128)S(1)} all-reduce(f32[2,2]{1,0:T(2,128)S(1)} %psum.30), channel_id=1, replica_groups=mesh['pix_0'=4,'pix_1'=8,'pix_2'=2,'band'=4] {'band'}, use_global_device_ids=true, to_apply=%region_19.20 | all-reduce | flops 4 | bytes 32 | tf_op jit(solution)/shard_map/psum | solution.py:17
  104.5 0.6 multiply_sqrt_fusion
  105.1 4.1 %sub.115 = f32[512,1024]{1,0:T(8,128)} subtract(f32[512,1024]{1,0:T(8,128)} %get-tuple-element.311, f32[512,1024]{1,0:T(8,128)} %get-tuple-element.155) | non-fusion elementwise | flops 524288 | bytes 6291456 | tf_op jit(solution)/shard_map/sub | solution.py:75
  (44 shorter events, 2.2 us)
Async XLA Ops:
  0.6 19.9 %copy-start = (f32[512,512]{1,0:T(8,128)S(1)}, f32[512,512]{1,0:T(8,128)}, u32[]{:S(2)}) copy-start(f32[512,512]{1,0:T(8,128)} %param.11) | copy-start | bytes 3145732
  2.5 17.5 %all-to-all-start = ((bf16[56,4,1024]{2,0,1:T(8,128)(2,1)}), bf16[56,4,1024]{2,0,1:T(8,128)(2,1)S(1)}, u32[]{:S(2)}, u32[]{:S(2)}) async-start(bf16[56,4,1024]{2,0,1:T(8,128)(2,1)} %bitcast.34), calls=%async_computation | async-start | bytes 917504 | tf_op jit(solution)/shard_map/all_to_all | solution.py:59
  20.5 8.7 %copy-start.2 = (f32[512,1024]{1,0:T(8,128)}, f32[512,1024]{1,0:T(8,128)S(1)}, u32[]{:S(2)}) copy-start(f32[512,1024]{1,0:T(8,128)S(1)} %fusion.29) | copy-start | bytes 6291460
  38.5 1.4 %copy-start.1 = (f32[512,1024]{1,0:T(8,128)}, f32[512,1024]{1,0:T(8,128)S(1)}, u32[]{:S(2)}) copy-start(f32[512,1024]{1,0:T(8,128)S(1)} %get-tuple-element.291) | copy-start | bytes 6291460
where the time goes:
time: 110 us; the launch traced here: 109 us
  blocking collectives  56.2 us (51%)
  other arithmetic  27.9 us (25%)
  matrix products  16.1 us (15%)
  starting transfers between devices  5 us (5%)
  local copies, waits for them, and re-layouts  2.93 us (3%)
    psum x4, blocking collectives, one_axis_at_a_time(): shard = lax.psum(shard, axis)  43.7 us
    dot_general x2, matrix products, body(): jnp.dot(gram_inverse, fit_term / penalty + current - scaled_dual, precisi...  15.7 us
    reduce_sum x14, other arithmetic, mass_at(): return jnp.sum(jnp.maximum(shifted - level[None, :], 0.0), axis=0)  13.3 us
    all_gather x1, blocking collectives, body(): all_rows = lax.all_gather(endmembers, 'band', axis=0, tiled=True)  12.5 us
    reduce_sum x1, other arithmetic, body(): primal_sum = jnp.sum((primal - updated) ** 2)  7.01 us
    all_to_all x1, starting transfers between devices, body(): lax.all_to_all(spectra, 'band', split_axis=1, concat_axis=0, tiled=True)  5 us
    sub x1, other arithmetic, body(): scaled_dual = scaled_dual + primal - updated  4.1 us
    another operation x2, other arithmetic, body(): totals = jnp.stack([jnp.stack(primal_list), jnp.stack(change_list)])  2.64 us
  transfers between devices with their start and end apart: 1, of which 0 were waited for; matrix products, arithmetic and copies ran while one was open for 0% of the time, Pallas kernels for 0%

commit v1 on v0

--- a/solution.py
+++ b/solution.py
@@ -56,7 +56,22 @@
 
 def body(spectra, endmembers, gram_inverse, abundances, duals):
     penalty = B / (2.0 * K * K)
-    exchanged = lax.all_to_all(spectra, "band", split_axis=1, concat_axis=0, tiled=True)
+    block_next = lax.psum(1, axis_name="band")
+    r2 = lax.axis_index("band")
+    outer, k_now = (block_next, r2)
+    base_arr = spectra.shape[1] // outer
+    odd = jnp.roll(spectra, -k_now * base_arr, axis=1)
+    finding = lax.slice_in_dim(odd, 0, base_arr, axis=1)
+    shelf = [finding]
+    for to_i in range(1, outer):
+        v_next = lax.slice_in_dim(odd, to_i * base_arr, (to_i + 1) * base_arr, axis=1)
+        shelf.append(
+            lax.ppermute(
+                v_next, axis_name="band", perm=[(jj, (jj + to_i) % outer) for jj in range(outer)]
+            )
+        )
+    earlier = jnp.concatenate(shelf[::-1], axis=0)
+    exchanged = jnp.roll(earlier, shift=(k_now + 1) * shelf[0].shape[0], axis=0)
     all_rows = lax.all_gather(endmembers, "band", axis=0, tiled=True)
     fit_term = contract_bands(all_rows, exchanged)
     fit_term = fit_term / K

time: 110 us -> 112 us (1.018)
  local copies, waits for them, and re-layouts: 2.93 us -> 17.7 us
  other arithmetic: 27.9 us -> 18.7 us
  blocking collectives: 56.2 us -> 54.2 us
  matrix products: 16.1 us -> 14.6 us
    unnamed x6 -> x25, local copies, waits for them, and re-layouts: 1.02 us -> 16 us
    reduce_sum x14, other arithmetic: 13.3 us -> 7.65 us  [mass_at(): return jnp.sum(jnp.maximum(shifted - level[None, :], 0.0), axis=0)]
    ppermute x0 -> x3, starting transfers between devices: none -> 5.22 us  [body(): lax.ppermute(v_next, axis_name='band', perm=[(jj, (jj + to_i) % outer) fo...]
    all_to_all x1 -> x0, starting transfers between devices: 5 us -> none  [body(): lax.all_to_all(spectra, 'band', split_axis=1, concat_axis=0, tiled=True)]
    sub x1 -> x0, other arithmetic: 4.1 us -> none  [body(): scaled_dual = scaled_dual + primal - updated]
    all_gather x1, blocking collectives: 12.5 us -> 10.2 us  [body(): all_rows = lax.all_gather(endmembers, 'band', axis=0, tiled=True)]
    all_to_all x1 -> x0, local copies, waits for them, and re-layouts: 1.9 us -> none  [body(): lax.all_to_all(spectra, 'band', split_axis=1, concat_axis=0, tiled=True)]
    dot_general x2, matrix products: 15.7 us -> 14.1 us  [body(): jnp.dot(gram_inverse, fit_term / penalty + current - scaled_dual, precisi...]
  transfers between devices with their start and end apart: 1 -> 3, of which waited for: 0 -> 0; matrix products, arithmetic and copies ran while one was open for 0% -> 5% of each run, Pallas kernels for 0% -> 0%
where the time goes in v1:
time: 112 us
  blocking collectives  54.2 us (48%)
  other arithmetic  18.7 us (17%)
  local copies, waits for them, and re-layouts  17.7 us (16%)
  matrix products  14.6 us (13%)
  starting transfers between devices  5.22 us (5%)
    psum x4, blocking collectives, one_axis_at_a_time(): shard = lax.psum(shard, axis)  44 us
    unnamed x25, local copies, waits for them, and re-layouts  16 us
    dot_general x2, matrix products, body(): jnp.dot(gram_inverse, fit_term / penalty + current - scaled_dual, precisi...  14.1 us
    all_gather x1, blocking collectives, body(): all_rows = lax.all_gather(endmembers, 'band', axis=0, tiled=True)  10.2 us
    reduce_sum x14, other arithmetic, mass_at(): return jnp.sum(jnp.maximum(shifted - level[None, :], 0.0), axis=0)  7.65 us
    reduce_sum x1, other arithmetic, body(): primal_sum = jnp.sum((primal - updated) ** 2)  6.42 us
    ppermute x3, starting transfers between devices, body(): lax.ppermute(v_next, axis_name='band', perm=[(jj, (jj + to_i) % outer) fo...  5.22 us
    another operation x2, other arithmetic, body(): totals = jnp.stack([jnp.stack(primal_list), jnp.stack(change_list)])  2.57 us
  transfers between devices with their start and end apart: 3, of which 0 were waited for; matrix products, arithmetic and copies ran while one was open for 5% of the time, Pallas kernels for 0%

profile of v1, /device:TPU:1, one launch (start us, length us, event | category | flops | bytes accessed | tf_op | source)
XLA Modules:
  0.0 111.6 jit_solution(9933235363385726759)
XLA Ops:
  0.7 1.3 %fusion.24 = bf16[56,4096]{1,0:T(8,128)(2,1)S(1)} fusion(s32[]{:T(128)S(6)} %select_n.49, bf16[56,4096]{1,0:T(8,128)(2,1)} %param.9), kind=kLoop, calls=%fused_computation.43 | loop fusion | flops 917504 | bytes 917508 | tf_op jit(solution)/shard_map/jit(_roll_dynamic)/concatenate | solution.py:63
  3.5 3.6 %collective-permute-start = (bf16[56,1024]{1,0:T(8,128)(2,1)}, bf16[56,1024]{1,0:T(8,128)(2,1)S(1)}, u32[]{:S(2)}, u32[]{:S(2)}) collective-permute-start(bf16[56,1024]{1,0:T(8,128)(2,1)} %get-tuple-element.186), channel_id=1, source_target_pairs={{0,3},{1,0},{2,1},{3,2},{4,7},{5,4},{6,5},{7,6},{8,11},{9,8},{10,9... | collective-permute-start | bytes 344072 | tf_op jit(solution)/shard_map/ppermute | solution.py:69
  7.1 1.7 %collective-permute-start.1 = (bf16[56,1024]{1,0:T(8,128)(2,1)}, bf16[56,1024]{1,0:T(8,128)(2,1)S(1)}, u32[]{:S(2)}, u32[]{:S(2)}) collective-permute-start(bf16[56,1024]{1,0:T(8,128)(2,1)} %get-tuple-element.185), channel_id=1, source_target_pairs={{0,2},{1,3},{2,0},{3,1},{4,6},{5,7},{6,4},{7,5},{8,10},{9,11},{10,... | collective-permute-start | bytes 344072 | tf_op jit(solution)/shard_map/ppermute | solution.py:69
  8.7 1.9 %copy.8 = f32[512,1024]{0,1:T(8,128)S(1)} copy(f32[512,1024]{1,0:T(8,128)} %param.12) | data formatting | bytes 4194304 | tf_op args[3]
  10.7 3.7 %copy.9 = f32[512,1024]{0,1:T(8,128)} copy(f32[512,1024]{1,0:T(8,128)} %param.13) | data formatting | bytes 4194304 | tf_op args[4]
  14.3 10.2 %all_gather.3 = bf16[224,512]{1,0:T(8,128)(2,1)S(1)} all-gather(bf16[56,512]{1,0:T(8,128)(2,1)S(1)} %copy-done.5), channel_id=1, replica_groups=mesh['pix_0'=4,'pix_1'=8,'pix_2'=2,'band'=4] {'band'}, dimensions={0}, use_global_device_ids=true | all-gather | bytes 286720 | tf_op jit(solution)/shard_map/all_gather | solution.py:75
  24.6 1.1 slice_dynamic-update-slice_fusion
  25.7 0.9 slice_dynamic-update-slice_fusion.1
  27.2 5.3 %fusion.33 = (f32[1024]{0:T(1024)S(1)}, f32[512,1024]{0,1:T(8,128)}, f32[1024,512]{1,0:T(8,128)}) fusion(f32[512,1024]{0,1:T(8,128)S(1)} %copy-done.3, f32[512,512]{1,0:T(8,128)S(1)} %copy-done, f32[512,1024]{0,1:T(8,128)S(1)} %copy.8, f32[1024,512]{1,0:T(8,128)S(1)} %fusion.25), kind=kOutput, calls=%fused_computation.68 | convolution fusion | flops 3223845888 | bytes 11538432 | tf_op jit(solution)/shard_map/dot_general | solution.py:84
  32.4 1.9 %copy.12 = f32[512,1024]{1,0:T(8,128)S(1)} copy(f32[512,1024]{0,1:T(8,128)} %get-tuple-element.173) | data formatting | bytes 4194304
  34.4 2.2 %maximum_reduce_fusion.3 = (f32[1024]{0:T(1024)S(1)}, f32[1024]{0:T(1024)S(1)}) fusion(f32[512,1024]{0,1:T(8,128)} %get-tuple-element.173, f32[1024]{0:T(1024)S(1)} %add_multiply_fusion.3), kind=kLoop, calls=%fused_computation.34 | loop fusion | flops 2095104 | bytes 2109440 | tf_op jit(solution)/shard_map/reduce_sum | solution.py:27
  36.5 1.9 %while.34 = (s32[]{:T(128)}, f32[1024]{0:T(1024)S(1)}, f32[1024]{0:T(1024)S(1)}, f32[1024]{0:T(1024)S(1)}, f32[1024]{0:T(1024)S(1)}, /*index=5*/f32[512,1024]{1,0:T(8,128)S(1)}, s32[]{:T(128)}, s32[]{:T(128)}) while((s32[]{:T(128)}, f32[1024]{0:T(1024)S(1)}, f32[1024]{0:T(1024)S(1)}, f32[1024]{0:T(1024)S(1)}, f32[1024]{0:T(1024)S(1)}, ...), condition=%wide.region_5.6_spmd.clone, body=%wide.region_3.5_spmd.clone.sunk | while | flops 1582083 | bytes 2154591 | solution.py:44
  38.5 8.9 %fusion.32 = (f32[1024]{0:T(1024)S(1)}, f32[512,1024]{0,1:T(8,128)}, f32[1024,512]{1,0:T(8,128)}) fusion(f32[512,1024]{0,1:T(8,128)} %get-tuple-element.173, f32[1024]{0:T(1024)S(1)} %divide_add_fusion.1, f32[512,512]{1,0:T(8,128)S(1)} %copy-done, f32[1024,512]{1,0:T(8,128)} %copy-done.2), kind=kOutput, calls=%fused_computation.67 | convolution fusion | flops 3226991616 | bytes 9445376 | tf_op jit(solution)/shard_map/dot_general | solution.py:84
  47.3 1.9 %copy.14 = f32[512,1024]{1,0:T(8,128)S(1)} copy(f32[512,1024]{0,1:T(8,128)} %get-tuple-element.171) | data formatting | bytes 4194304
  49.3 2.2 %maximum_reduce_fusion.2 = (f32[1024]{0:T(1024)S(1)}, f32[1024]{0:T(1024)S(1)}) fusion(f32[512,1024]{0,1:T(8,128)} %get-tuple-element.171, f32[1024]{0:T(1024)S(1)} %add_multiply_fusion.2), kind=kLoop, calls=%fused_computation.31 | loop fusion | flops 2095104 | bytes 2109440 | tf_op jit(solution)/shard_map/reduce_sum | solution.py:27
  51.4 1.9 %while.35 = (s32[]{:T(128)}, f32[1024]{0:T(1024)S(1)}, f32[1024]{0:T(1024)S(1)}, f32[1024]{0:T(1024)S(1)}, f32[1024]{0:T(1024)S(1)}, /*index=5*/f32[512,1024]{1,0:T(8,128)S(1)}, s32[]{:T(128)}, s32[]{:T(128)}) while((s32[]{:T(128)}, f32[1024]{0:T(1024)S(1)}, f32[1024]{0:T(1024)S(1)}, f32[1024]{0:T(1024)S(1)}, ...), condition=%wide.region_11.12_spmd.clone, body=%wide.region_9.11_spmd.clone.sunk | while | flops 1582083 | bytes 2154591 | solution.py:44
  53.4 6.4 %fusion.9 = (f32[]{:T(128)}, f32[]{:T(128)}, f32[]{:T(128)}, f32[]{:T(128)}, f32[512,1024]{0,1:T(8,128)}, /*index=5*/f32[512,1024]{0,1:T(8,128)S(1)}) fusion(f32[1024,512]{1,0:T(8,128)} %get-tuple-element.187, f32[512,1024]{0,1:T(8,128)} %get-tuple-element.173, f32[1024]{0:T(1024)S(1)} %divide_add_fusion.1, f32[512,1024]{0,1:T(8,128)} %copy-done.1, ...), kind=kLoop, calls=%fused_computation.21 | loop fusion | flops 8912892 | bytes 14688272 | tf_op jit(solution)/shard_map/reduce_sum | solution.py:91
  59.8 2.6 %maximum_bitcast_fusion = (f32[1,2]{1,0:T(1,128)S(1)}, f32[1,2]{1,0:T(1,128)S(1)}) fusion(f32[1]{0:T(128)} %bitcast.4, f32[1]{0:T(128)} %bitcast.3, f32[1]{0:T(128)} %bitcast.7, f32[1]{0:T(128)} %bitcast.6), kind=kLoop, calls=%fused_computation.61 | loop fusion | flops 4 | bytes 32 | tf_op jit(solution)/shard_map/stack | solution.py:96
  62.3 8.5 %psum.28 = f32[2,2]{1,0:T(2,128)S(1)} all-reduce(f32[2,2]{1,0:T(2,128)S(1)} %pad_maximum_fusion), channel_id=1, replica_groups=mesh['pix_0'=4,'pix_1'=8,'pix_2'=2,'band'=4] {'pix_0'}, use_global_device_ids=true, to_apply=%region_16.17 | all-reduce | flops 4 | bytes 32 | tf_op jit(solution)/shard_map/psum | solution.py:17
  70.8 16.2 %psum.29 = f32[2,2]{1,0:T(2,128)S(1)} all-reduce(f32[2,2]{1,0:T(2,128)S(1)} %psum.28), channel_id=1, replica_groups=mesh['pix_0'=4,'pix_1'=8,'pix_2'=2,'band'=4] {'pix_1'}, use_global_device_ids=true, to_apply=%region_17.18 | all-reduce | flops 4 | bytes 32 | tf_op jit(solution)/shard_map/psum | solution.py:17
  87.1 11.6 %psum.30 = f32[2,2]{1,0:T(2,128)S(1)} all-reduce(f32[2,2]{1,0:T(2,128)S(1)} %psum.29), channel_id=1, replica_groups=mesh['pix_0'=4,'pix_1'=8,'pix_2'=2,'band'=4] {'pix_2'}, use_global_device_ids=true, to_apply=%region_18.19 | all-reduce | flops 4 | bytes 32 | tf_op jit(solution)/shard_map/psum | solution.py:17
  98.7 2.9 %copy.16 = f32[512,1024]{1,0:T(8,128)} copy(f32[512,1024]{0,1:T(8,128)} %get-tuple-element.182) | data formatting | bytes 4194304
  101.5 7.7 %psum.31 = f32[2,2]{1,0:T(2,128)S(1)} all-reduce(f32[2,2]{1,0:T(2,128)S(1)} %psum.30), channel_id=1, replica_groups=mesh['pix_0'=4,'pix_1'=8,'pix_2'=2,'band'=4] {'band'}, use_global_device_ids=true, to_apply=%region_19.20 | all-reduce | flops 4 | bytes 32 | tf_op jit(solution)/shard_map/psum | solution.py:17
  109.8 1.8 %copy.17 = f32[512,1024]{1,0:T(8,128)} copy(f32[512,1024]{0,1:T(8,128)S(1)} %get-tuple-element.183) | data formatting | bytes 4194304
  (68 shorter events, 6.2 us)
Async XLA Ops:
  0.6 26.5 %copy-start = (f32[512,512]{1,0:T(8,128)S(1)}, f32[512,512]{1,0:T(8,128)}, u32[]{:S(2)}) copy-start(f32[512,512]{1,0:T(8,128)} %param.11) | copy-start | bytes 3145732
  2.0 0.8 copy-start.4
  3.5 21.1 %collective-permute-start = (bf16[56,1024]{1,0:T(8,128)(2,1)}, bf16[56,1024]{1,0:T(8,128)(2,1)S(1)}, u32[]{:S(2)}, u32[]{:S(2)}) collective-permute-start(bf16[56,1024]{1,0:T(8,128)(2,1)} %get-tuple-element.186), channel_id=1, source_target_pairs={{0,3},{1,0},{2,1},{3,2},{4,7},{5,4},{6,5},{7,6},{8,11},{9,8},{10,9... | collective-permute-start | bytes 344072 | tf_op jit(solution)/shard_map/ppermute | solution.py:69
  7.1 17.6 %collective-permute-start.2 = (bf16[56,1024]{1,0:T(8,128)(2,1)}, bf16[56,1024]{1,0:T(8,128)(2,1)S(1)}, u32[]{:S(2)}, u32[]{:S(2)}) collective-permute-start(bf16[56,1024]{1,0:T(8,128)(2,1)} %get-tuple-element.184), channel_id=1, source_target_pairs={{0,1},{1,2},{2,3},{3,0},{4,5},{5,6},{6,7},{7,4},{8,9},{9,10},{10,1... | collective-permute-start | bytes 344072 | tf_op jit(solution)/shard_map/ppermute | solution.py:69
  7.1 17.5 %collective-permute-start.1 = (bf16[56,1024]{1,0:T(8,128)(2,1)}, bf16[56,1024]{1,0:T(8,128)(2,1)S(1)}, u32[]{:S(2)}, u32[]{:S(2)}) collective-permute-start(bf16[56,1024]{1,0:T(8,128)(2,1)} %get-tuple-element.185), channel_id=1, source_target_pairs={{0,2},{1,3},{2,0},{3,1},{4,6},{5,7},{6,4},{7,5},{8,10},{9,11},{10,... | collective-permute-start | bytes 344072 | tf_op jit(solution)/shard_map/ppermute | solution.py:69
  10.6 16.5 %copy-start.1 = (f32[512,1024]{0,1:T(8,128)}, f32[512,1024]{0,1:T(8,128)S(1)}, u32[]{:S(2)}) copy-start(f32[512,1024]{0,1:T(8,128)S(1)} %copy.8) | copy-start | bytes 6291460
  10.7 3.7 %copy-start.5 = (bf16[56,512]{1,0:T(8,128)(2,1)S(1)}, bf16[56,512]{1,0:T(8,128)(2,1)}, u32[]{:S(2)}) copy-start(bf16[56,512]{1,0:T(8,128)(2,1)} %param.10) | copy-start | bytes 172036
  24.6 2.5 %copy-start.3 = (f32[512,1024]{0,1:T(8,128)S(1)}, f32[512,1024]{0,1:T(8,128)}, u32[]{:S(2)}) copy-start(f32[512,1024]{0,1:T(8,128)} %copy.9) | copy-start | bytes 6291460
  27.2 5.3 %copy-start.2 = (f32[1024,512]{1,0:T(8,128)}, f32[1024,512]{1,0:T(8,128)S(1)}, u32[]{:S(2)}) copy-start(f32[1024,512]{1,0:T(8,128)S(1)} %fusion.25) | copy-start | bytes 6291460
